TPU v7x, 32 devices: a whole 2x2x4 slice. The times are simulated.
32 devices in a mesh: groups: 2 (over y), width: 4 (over z), hidden: 2 (over x), batch: 2 (over core).
Axes of the slice: x: 2, y: 2, z: 4, core: 2. Of those that a mesh axis runs over, the one named last changes fastest.
Arguments:
- inputs: bfloat16 [2, 32, 16384], P(None, 'groups', 'width'), parts along dimension 1, may hold values from -42 to 42
- norm_gain: float32 [16384], P('width'), may hold values from 0.25 to 1.75
- wq_packed: int32 [16384, 4096], P('width', 'hidden'), may hold values from 0 to 255, as said below
- wq_scales: float32 [128, 8192], P('width', 'hidden'), may hold values from 0.002578125 to 0.01015625
- key_weight: bfloat16 [16384, 512], P('width', 'hidden'), may hold values from -0.046875 to 0.046875
- value_weight: bfloat16 [16384, 512], P('width', 'hidden'), may hold values from -0.046875 to 0.046875
- wo_weight: bfloat16 [8192, 16384], P('hidden', 'width'), may hold values from -0.3125 to 0.3125
- key_cache: bfloat16 [32, 1024, 512], P(('groups', 'width', 'batch'), None, 'hidden'), parts along dimension 0, may hold values from -6 to 6
- value_cache: bfloat16 [32, 1024, 512], P(('groups', 'width', 'batch'), None, 'hidden'), parts along dimension 0, may hold values from -6 to 6
- lengths: int32 [32], P(('groups', 'width', 'batch')), parts along dimension 0, may hold values from 256 to 1022, as said below
Outputs:
- attended: bfloat16 [2, 32, 16384], P(None, ('groups', 'hidden', 'batch'), 'width'), parts along dimension 1
There are 2 independent parts, one for each index of `groups`. A program takes and returns all parts, laid end to end along the dimension named above; an argument that names none is the same for every part. Nothing has to cross between parts.
Inputs may be any that keep to these rules, and one draw needn't show every extreme that they name: `wq_packed`: each word holds two 4-bit codes, bits 4 c to 4 c + 3 for column 2 j + c. `lengths`: some sequence has exactly 1022 filled slots.
All inputs are finite; a program needn't handle non-finite values.
Results may differ from a plain program's by a relative error of at most 0.0091.
Values may be sent and summed in bfloat16 or wider, within the bound.
No kernel may reach another device: no remote copies, remote signals or barrier semaphores. Data moves between devices by JAX's collectives and lax.ppermute only.
A program may use at most 448 MiB of HBM per device.

v0:
```python
import jax
import jax.numpy as jnp
from jax import lax
from jax.sharding import PartitionSpec as P

D = 16384
HEAD = 128
STEPS = 2


def unpack_weights(packed, scales, bits, per_word):
    shifts = jnp.arange(per_word, dtype=jnp.int32) * bits
    codes = packed[:, :, None] >> shifts & (1 << bits) - 1
    values = (codes - (1 << bits - 1)).astype(jnp.float32)
    values = values.reshape(packed.shape[0], packed.shape[1] * per_word)
    group_rows = packed.shape[0] // scales.shape[0]
    values = values.reshape(scales.shape[0], group_rows, values.shape[1]) * scales[:, None, :]
    return values.reshape(packed.shape[0], -1)


def rotate_heads(field, positions):
    half = field.shape[-1] // 2
    freq = 500000.0 ** (-2.0 * jnp.arange(half, dtype=jnp.float32) / field.shape[-1])
    angle = positions.astype(jnp.float32)[:, None] * freq[None, :]
    cosine = jnp.cos(angle)[:, None, :]
    sine = jnp.sin(angle)[:, None, :]
    first = field[..., :half]
    second = field[..., half:]
    return jnp.concatenate(
        [first * cosine - second * sine, second * cosine + first * sine], axis=-1
    )


def on_device(
    inputs,
    norm_gain,
    wq_packed,
    wq_scales,
    key_weight,
    value_weight,
    wo_weight,
    key_cache,
    value_cache,
    lengths,
):
    high = lax.Precision.HIGHEST
    w_query = unpack_weights(wq_packed, wq_scales, 4, 2)
    w_output = wo_weight.astype(jnp.float32)
    w_joined = jnp.concatenate(
        [w_query, key_weight.astype(jnp.float32), value_weight.astype(jnp.float32)], axis=1
    )
    seq_local = lengths.shape[0]
    slots = key_cache.shape[1]
    kv_local = key_weight.shape[1] // HEAD
    q_local = w_query.shape[1] // HEAD
    repeat = q_local // kv_local
    cols_local = inputs.shape[2]
    keys_all = key_cache
    values_all = value_cache
    slot_ids = jnp.arange(slots, dtype=jnp.int32)
    results = []
    for step in range(STEPS):
        rows = inputs[step].astype(jnp.float32)
        width_count = lax.axis_size("width")
        batch_count = lax.axis_size("batch")
        arranged = rows.reshape(width_count, batch_count, seq_local, cols_local)
        rows = lax.dynamic_index_in_dim(arranged, lax.axis_index("batch"), 1, keepdims=False)
        rows = rows.reshape(width_count * seq_local, cols_local)
        squares = jnp.sum(rows * rows, axis=1)
        total = lax.psum(squares, "width")
        scale = lax.rsqrt(total / D + 1e-05)
        normed = rows * scale[:, None] * norm_gain[None, :]
        partial_value = jnp.dot(
            normed, w_joined, precision=high, preferred_element_type=jnp.float32
        )
        terms = (partial_value,)
        summed = (lax.psum_scatter(terms[0], "width", scatter_dimension=0, tiled=True),)
        projected = summed[0]
        positions = lengths + step
        q_cols = q_local * HEAD
        kv_cols = kv_local * HEAD
        queries = rotate_heads(
            projected[:, :q_cols].reshape(seq_local, q_local, HEAD), positions
        ).astype(jnp.bfloat16)
        keys_new = rotate_heads(
            projected[:, q_cols : q_cols + kv_cols].reshape(seq_local, kv_local, HEAD), positions
        )
        keys_new = keys_new.reshape(seq_local, kv_cols).astype(jnp.bfloat16)
        values_new = projected[:, q_cols + kv_cols :].astype(jnp.bfloat16)
        written = slot_ids[None, :, None] == positions[:, None, None]
        keys_all = jnp.where(written, keys_new[:, None, :], keys_all)
        values_all = jnp.where(written, values_new[:, None, :], values_all)
        query_heads = queries.reshape(seq_local, kv_local, repeat, HEAD)
        key_heads = keys_all.reshape(seq_local, slots, kv_local, HEAD)
        value_heads = values_all.reshape(seq_local, slots, kv_local, HEAD)
        scores = jnp.einsum(
            "bgrd,bsgd->bgrs", query_heads, key_heads, preferred_element_type=jnp.float32
        ) * HEAD ** (-0.5)
        valid = slot_ids[None, None, None, :] <= positions[:, None, None, None]
        scores = jnp.where(valid, scores, -1e30)
        peak = jnp.max(scores, axis=-1, keepdims=True)
        weights = jnp.exp(scores - peak)
        total_weight = jnp.sum(weights, axis=-1, keepdims=True)
        probs = (weights / total_weight).astype(jnp.bfloat16)
        mixed = jnp.einsum(
            "bgrs,bsgd->bgrd", probs, value_heads, preferred_element_type=jnp.float32
        )
        mixed = mixed.reshape(seq_local, q_cols).astype(jnp.bfloat16)
        out_terms = jnp.dot(
            lax.all_gather(mixed, ("width", "batch"), axis=0, tiled=True).astype(jnp.float32),
            w_output,
            precision=high,
            preferred_element_type=jnp.float32,
        )
        head_sums = lax.psum_scatter(out_terms, "hidden", scatter_dimension=0, tiled=True)
        share = head_sums.shape[0] // lax.axis_size("batch")
        attended = lax.dynamic_slice_in_dim(head_sums, lax.axis_index("batch") * share, share, 0)
        results.append(attended.astype(jnp.bfloat16))
    return jnp.stack(results)


def solution(mesh):
    in_specs = (
        P(None, "groups", "width"),
        P("width"),
        P("width", "hidden"),
        P("width", "hidden"),
        P("width", "hidden"),
        P("width", "hidden"),
        P("hidden", "width"),
        P(("groups", "width", "batch"), None, "hidden"),
        P(("groups", "width", "batch"), None, "hidden"),
        P(("groups", "width", "batch")),
    )
    out_specs = P(None, ("groups", "hidden", "batch"), "width")
    return jax.shard_map(
        on_device, mesh=mesh, in_specs=in_specs, out_specs=out_specs, check_vma=False
    )
```

profile of v0, /device:TPU:0, one launch (start us, length us, event | category | flops | bytes accessed | tf_op | source)
XLA Modules:
  0.0 575.9 jit_solution(8795833345152713637)
XLA Ops:
  6.5 1.0 slice_convert_fusion.1
  8.2 13.4 %all-reduce.2 = (f32[8]{0:T(128)S(1)}, f32[8]{0:T(128)S(1)}) all-reduce(f32[8]{0:T(128)S(1)} %reduce_sum.44, f32[8]{0:T(128)S(1)} %reduce_sum.41), channel_id=1, replica_groups=mesh['groups'=2,'width'=4,'hidden'=2,'batch'=2] {'width'}, use_global_device_ids=true, to_apply=%region_7.8 | all-reduce | flops 16 | bytes 128 | tf_op jit(solution)/shard_map/psum | solution.py:70
  22.2 0.7 reshape.281
  22.9 31.1 %copy.23 = s32[4096,2048]{0,1:T(8,128)} copy(s32[4096,2048]{1,0:T(8,128)} %param.12) | data formatting | bytes 67108864 | tf_op args[2]
  54.0 39.8 %shift_right_arithmetic.21 = s32[4096,2048,2]{0,2,1:T(2,128)} broadcast(s32[4096,2048]{0,1:T(8,128)} %copy.23), dimensions={0,1} | broadcast | bytes 100663296 | tf_op jit(solution)/shard_map/shift_right_arithmetic | solution.py:13
  93.8 78.3 %shift_right_arithmetic.22 = s32[4096,4096]{0,1:T(8,128)} reshape(s32[4096,2048,2]{0,2,1:T(2,128)} %shift_right_arithmetic.21) | data formatting | bytes 134217728 | tf_op jit(solution)/shard_map/shift_right_arithmetic | solution.py:13
  173.3 4.1 copy.25
  177.4 4.0 convert_element_type.85
  181.4 4.1 copy.26
  185.5 4.1 convert_element_type.86
  189.7 41.1 %mul.120 = f32[32,128,4096]{1,0,2:T(8,128)} broadcast(f32[32,4096]{0,1:T(8,128)S(1)} %copy.24), dimensions={0,2} | broadcast | bytes 67633152 | tf_op jit(solution)/shard_map/mul | solution.py:17
  230.7 79.0 %bitcast_multiply_fusion = f32[4096,4096]{0,1:T(8,128)} fusion(f32[512,8,32,128]{3,2,1,0:T(8,128)} %bitcast.17, s32[4096,4096]{0,1:T(8,128)} %shift_right_arithmetic.22, s32[4096]{0:T(1024)S(1)} %shift_right_arithmetic.24), kind=kLoop, calls=%fused_computation.3 | loop fusion | flops 83886080 | bytes 201342976 | tf_op jit(solution)/shard_map/mul | solution.py:17
  309.8 78.8 %fusion.3 = f32[8,4608]{1,0:T(8,128)} fusion(f32[4096,256]{0,1:T(8,128)} %convert_element_type.86, f32[4096,256]{0,1:T(8,128)} %convert_element_type.85, f32[4096,4096]{0,1:T(8,128)} %bitcast_multiply_fusion, f32[8,4096]{1,0:T(8,128)S(1)} %copy-done.5, f32[4096]{0:T(1024)S(1)} %copy-done.7, f32[8]{0:T(128)S(1)} %copy-done.9), kind=kOutput, calls=%fused_computation.5 | convolution fusion | flops 1849753600 | bytes 75792416 | tf_op jit(solution)/shard_map/dot_general | solution.py:73
  388.6 65.2 %fusion.2 = f32[8,4608]{1,0:T(8,128)} fusion(f32[4096,256]{0,1:T(8,128)S(1)} %copy-done.1, f32[4096,256]{0,1:T(8,128)S(1)} %copy-done, f32[4096,4096]{0,1:T(8,128)} %bitcast_multiply_fusion, f32[8,4096]{1,0:T(8,128)S(1)} %reshape.286, f32[8]{0:T(128)S(1)} %add_rsqrt_fusion, f32[4096]{0:T(1024)S(1)} %copy-done.7), kind=kOutput, calls=%fused_computation.4 | convolution fusion | flops 1849753600 | bytes 75792416 | tf_op jit(solution)/shard_map/dot_general | solution.py:73
  455.4 32.9 %all-reduce.6.cloned.1.call-done = (f32[8,4608]{1,0:T(8,128)}, f32[8,4608]{1,0:T(8,128)}) async-done(((f32[8,4608]{1,0:T(8,128)}, f32[8,4608]{1,0:T(8,128)}), (f32[8,4608]{1,0:T(8,128)}, f32[8,4608]{1,0:T(8,128)})) %all-reduce.6.cloned.1.call-update) | async-done | bytes 294928
  488.3 0.8 dynamic-slice.8
  489.0 0.8 dynamic-slice.5
  489.8 0.8 dynamic-slice.14
  490.6 0.8 dynamic-slice.15
  491.4 0.9 dynamic-slice_bitcast_fusion.1
  492.3 0.9 dynamic-slice_bitcast_fusion
  493.7 2.4 fusion.19
  496.7 1.6 convolution_convert_fusion.1
  498.3 14.0 %all-gather = bf16[8,2,4096]{2,1,0:T(2,128)(2,1)S(1)} all-gather(bf16[1,2,4096]{2,1,0:T(2,128)(2,1)S(1)} %reshape.293), channel_id=1, replica_groups=mesh['groups'=2,'width'=4,'hidden'=2,'batch'=2] {'width','batch'}, dimensions={0}, use_global_device_ids=true | all-gather | bytes 147456 | tf_op jit(solution)/shard_map/all_gather | solution.py:110
  512.3 13.8 %fusion.48 = f32[16,4096]{1,0:T(8,128)} fusion(bf16[16,4096]{1,0:T(8,128)(2,1)S(1)} %reshape.294, bf16[4096,4096]{1,0:T(8,128)(2,1)} %param.16), kind=kOutput, calls=%fused_computation.100 | convolution fusion | flops 536870912 | bytes 33947648 | tf_op jit(solution)/shard_map/dot_general | solution.py:109
  526.9 1.6 convolution_convert_fusion
  528.5 14.0 %all-gather.1 = bf16[8,2,4096]{2,1,0:T(2,128)(2,1)S(1)} all-gather(bf16[1,2,4096]{2,1,0:T(2,128)(2,1)S(1)} %reshape.295), channel_id=1, replica_groups=mesh['groups'=2,'width'=4,'hidden'=2,'batch'=2] {'width','batch'}, dimensions={0}, use_global_device_ids=true | all-gather | bytes 147456 | tf_op jit(solution)/shard_map/all_gather | solution.py:110
  542.5 13.5 %fusion.49 = f32[16,4096]{1,0:T(8,128)} fusion(bf16[16,4096]{1,0:T(8,128)(2,1)S(1)} %reshape.296, bf16[4096,4096]{1,0:T(8,128)(2,1)} %param.16), kind=kOutput, calls=%fused_computation.101 | convolution fusion | flops 536870912 | bytes 33947648 | tf_op jit(solution)/shard_map/dot_general | solution.py:109
  556.1 0.9 fusion.30
  557.1 10.7 %reduce-scatter.5.cloned.1.call-done = f32[8,4096]{1,0:T(8,128)} async-done(((f32[16,4096]{1,0:T(8,128)}), f32[8,4096]{1,0:T(8,128)}) %reduce-scatter.5.cloned.1.call-update) | async-done | bytes 131088 | tf_op jit(solution)/shard_map/reduce_scatter | solution.py:115
  567.7 0.9 fusion.31
  568.7 0.7 pad_maximum_fusion.3
  (64 shorter events, 5.4 us)
Async XLA Ops:
  6.5 481.7 %all-reduce.6.cloned.1.call-start = ((), (), s32[]{:S(2)}) async-start(), calls=%async_computation.4 | async-start | bytes 589824
  93.8 78.3 %copy-start.4 = (f32[32,4096]{1,0:T(8,128)S(1)}, f32[32,4096]{1,0:T(8,128)}, u32[]{:S(2)}) copy-start(f32[32,4096]{1,0:T(8,128)} %param.13) | copy-start | bytes 1572868
  230.7 79.0 %copy-start.5 = (f32[8,4096]{1,0:T(8,128)S(1)}, f32[8,4096]{1,0:T(8,128)}, u32[]{:S(2)}) copy-start(f32[8,4096]{1,0:T(8,128)} %reshape.281) | copy-start | bytes 393220
  230.7 79.0 %copy-start.7 = (f32[4096]{0:T(1024)S(1)}, f32[4096]{0:T(1024)}, u32[]{:S(2)}) copy-start(f32[4096]{0:T(1024)} %param.11) | copy-start | bytes 49156
  230.7 79.0 %copy-start.9 = (f32[8]{0:T(128)S(1)}, f32[8]{0:T(128)}, u32[]{:S(2)}) copy-start(f32[8]{0:T(128)} %add_rsqrt_fusion.1) | copy-start | bytes 100
  309.8 78.8 %copy-start = (f32[4096,256]{0,1:T(8,128)S(1)}, f32[4096,256]{0,1:T(8,128)}, u32[]{:S(2)}) copy-start(f32[4096,256]{0,1:T(8,128)} %convert_element_type.85) | copy-start | bytes 12582916
  309.8 78.8 %copy-start.1 = (f32[4096,256]{0,1:T(8,128)S(1)}, f32[4096,256]{0,1:T(8,128)}, u32[]{:S(2)}) copy-start(f32[4096,256]{0,1:T(8,128)} %convert_element_type.86) | copy-start | bytes 12582916
  388.5 65.4 %copy-start.6 = (s32[2]{0:T(128)S(1)}, s32[2]{0:T(128)}, u32[]{:S(2)}) copy-start(s32[2]{0:T(128)} %param.19) | copy-start | bytes 28
  388.5 65.5 %copy-start.8 = (u32[32]{0:T(128)S(1)}, u32[32]{0:T(128)}, u32[]{:S(2)}) copy-start(u32[32]{0:T(128)} %constant.51) | copy-start | bytes 388
  388.5 105.1 %copy-start.2 = (bf16[2,1024,256]{2,1,0:T(8,128)(2,1)S(1)}, bf16[2,1024,256]{2,1,0:T(8,128)(2,1)}, u32[]{:S(2)}) copy-start(bf16[2,1024,256]{2,1,0:T(8,128)(2,1)} %param.18) | copy-start | bytes 3145732
  388.6 105.1 %copy-start.3 = (bf16[2,1024,256]{2,1,0:T(8,128)(2,1)S(1)}, bf16[2,1024,256]{2,1,0:T(8,128)(2,1)}, u32[]{:S(2)}) copy-start(bf16[2,1024,256]{2,1,0:T(8,128)(2,1)} %param.17) | copy-start | bytes 3145732
  453.8 102.3 %reduce-scatter.3.cloned.1.call-start = ((), (), s32[]{:S(2)}) async-start(), calls=%async_computation.2 | async-start | bytes 393216 | tf_op jit(solution)/shard_map/reduce_scatter | solution.py:115
  526.1 41.6 %reduce-scatter.5.cloned.1.call-start = ((), (), s32[]{:S(2)}) async-start(), calls=%async_computation.3 | async-start | bytes 393216 | tf_op jit(solution)/shard_map/reduce_scatter | solution.py:115
Sparse Core Ops, SparseCore 0:
  454.0 34.2 all-reduce.5
  526.3 11.4 reduce-scatter.2
  556.2 11.4 reduce-scatter.4
where the time goes:
time: 579 us; the launch traced here: 576 us
  local copies, waits for them, and re-layouts  209 us (36%)
  matrix products  175 us (30%)
  other arithmetic  93 us (16%)
  waiting for transfers between devices  43.6 us (8%)
  blocking collectives  41.4 us (7%)
  between operations  14 us (2%)
    dot_general x2, matrix products, on_device(): jnp.dot(normed, w_joined, precision=high, preferred_element_type=jnp.floa...  144 us
    shift_right_arithmetic x4, local copies, waits for them, and re-layouts, unpack_weights(): codes = packed[:, :, None] >> shifts & (1 << bits) - 1  119 us
    mul x1, other arithmetic, unpack_weights(): values.reshape(scales.shape[0], group_rows, values.shape[1])  79 us
    unnamed x35, local copies, waits for them, and re-layouts  42.6 us
    mul x1, local copies, waits for them, and re-layouts, unpack_weights(): values.reshape(scales.shape[0], group_rows, values.shape[1])  41.1 us
    unnamed x4, waiting for transfers between devices  32.9 us
    all_gather x2, blocking collectives, on_device(): lax.all_gather(mixed, ('width', 'batch'), axis=0, tiled=True)  28 us
    dot_general x2, matrix products, on_device(): jnp.dot(lax.all_gather(mixed, ('width', 'batch'), axis=0, tiled=True).ast...  27.3 us
  transfers between devices with their start and end apart: 3, of which 2 were waited for; matrix products, arithmetic and copies ran while one was open for 3% of the time, Pallas kernels for 0%

commit v1 on v0

--- a/solution.py
+++ b/solution.py
@@ -67,7 +67,9 @@
         rows = lax.dynamic_index_in_dim(arranged, lax.axis_index("batch"), 1, keepdims=False)
         rows = rows.reshape(width_count * seq_local, cols_local)
         squares = jnp.sum(rows * rows, axis=1)
-        total = lax.psum(squares, "width")
+        total = squares
+        for hop in (1, 2):
+            total = total + lax.ppermute(total, "width", [(dev, dev ^ hop) for dev in range(4)])
         scale = lax.rsqrt(total / D + 1e-05)
         normed = rows * scale[:, None] * norm_gain[None, :]
         partial_value = jnp.dot(

time: 579 us -> 578 us (level)
  blocking collectives: 41.4 us -> 28 us
  starting transfers between devices: 0.09 us -> 6.57 us
    psum x1 -> x0, blocking collectives: 13.4 us -> none  [on_device(): total = lax.psum(squares, 'width')]
    ppermute x0 -> x4, starting transfers between devices: none -> 6.49 us  [on_device(): lax.ppermute(total, 'width', [(dev, dev ^ hop) for dev in range(4)])]
  transfers between devices with their start and end apart: 3 -> 7, of which waited for: 2 -> 3; matrix products, arithmetic and copies ran while one was open for 3% -> 67% of each run, Pallas kernels for 0% -> 0%
where the time goes in v1:
time: 578 us; the launch traced here: 575 us
  local copies, waits for them, and re-layouts  210 us (36%)
  matrix products  175 us (30%)
  other arithmetic  94.5 us (16%)
  waiting for transfers between devices  47.4 us (8%)
  blocking collectives  28 us (5%)
  between operations  14 us (2%)
  starting transfers between devices  6.57 us (1%)
    dot_general x2, matrix products, on_device(): jnp.dot(normed, w_joined, precision=high, preferred_element_type=jnp.floa...  144 us
    shift_right_arithmetic x4, local copies, waits for them, and re-layouts, unpack_weights(): codes = packed[:, :, None] >> shifts & (1 << bits) - 1  119 us
    mul x1, other arithmetic, unpack_weights(): values.reshape(scales.shape[0], group_rows, values.shape[1])  79 us
    unnamed x35, local copies, waits for them, and re-layouts  42.6 us
    mul x1, local copies, waits for them, and re-layouts, unpack_weights(): values.reshape(scales.shape[0], group_rows, values.shape[1])  41 us
    unnamed x4, waiting for transfers between devices  36.3 us
    all_gather x2, blocking collectives, on_device(): lax.all_gather(mixed, ('width', 'batch'), axis=0, tiled=True)  28 us
    dot_general x2, matrix products, on_device(): jnp.dot(lax.all_gather(mixed, ('width', 'batch'), axis=0, tiled=True).ast...  27.3 us
  transfers between devices with their start and end apart: 7, of which 3 were waited for; matrix products, arithmetic and copies ran while one was open for 67% of the time, Pallas kernels for 0%

profile of v1, /device:TPU:0, one launch (start us, length us, event | category | flops | bytes accessed | tf_op | source)
XLA Modules:
  0.0 575.1 jit_solution(14285009847147021850)
XLA Ops:
  6.5 1.0 slice_convert_fusion.1
  8.7 3.0 collective-permute-start
  13.6 31.2 %copy.23 = s32[4096,2048]{0,1:T(8,128)} copy(s32[4096,2048]{1,0:T(8,128)} %param.12) | data formatting | bytes 67108864 | tf_op args[2]
  44.8 39.8 %shift_right_arithmetic.21 = s32[4096,2048,2]{0,2,1:T(2,128)} broadcast(s32[4096,2048]{0,1:T(8,128)} %copy.23), dimensions={0,1} | broadcast | bytes 100663296 | tf_op jit(solution)/shard_map/shift_right_arithmetic | solution.py:13
  84.6 78.3 %shift_right_arithmetic.22 = s32[4096,4096]{0,1:T(8,128)} reshape(s32[4096,2048,2]{0,2,1:T(2,128)} %shift_right_arithmetic.21) | data formatting | bytes 134217728 | tf_op jit(solution)/shard_map/shift_right_arithmetic | solution.py:13
  164.0 4.1 copy.25
  168.1 4.0 convert_element_type.85
  172.2 4.1 copy.26
  176.3 4.0 convert_element_type.86
  180.4 41.0 %mul.120 = f32[32,128,4096]{1,0,2:T(8,128)} broadcast(f32[32,4096]{0,1:T(8,128)S(1)} %copy.24), dimensions={0,2} | broadcast | bytes 67633152 | tf_op jit(solution)/shard_map/mul | solution.py:17
  221.5 79.0 %bitcast_multiply_fusion = f32[4096,4096]{0,1:T(8,128)} fusion(f32[512,8,32,128]{3,2,1,0:T(8,128)} %bitcast.17, s32[4096,4096]{0,1:T(8,128)} %shift_right_arithmetic.22, s32[4096]{0:T(1024)S(1)} %shift_right_arithmetic.24), kind=kLoop, calls=%fused_computation.3 | loop fusion | flops 83886080 | bytes 201342976 | tf_op jit(solution)/shard_map/mul | solution.py:17
  300.5 0.8 add.54
  301.3 3.1 collective-permute-start.1
  305.9 78.6 %fusion.3 = f32[8,4608]{1,0:T(8,128)} fusion(f32[4096,256]{0,1:T(8,128)} %convert_element_type.86, f32[4096,256]{0,1:T(8,128)} %convert_element_type.85, f32[4096,4096]{0,1:T(8,128)} %bitcast_multiply_fusion, f32[8,4096]{1,0:T(8,128)S(1)} %copy-done.5, f32[4096]{0:T(1024)S(1)} %copy-done.8, f32[8]{0:T(128)S(1)} %add_rsqrt_fusion.1), kind=kOutput, calls=%fused_computation.5 | convolution fusion | flops 1849753600 | bytes 75792416 | tf_op jit(solution)/shard_map/dot_general | solution.py:75
  384.6 65.2 %fusion.2 = f32[8,4608]{1,0:T(8,128)} fusion(f32[4096,256]{0,1:T(8,128)S(1)} %copy-done.1, f32[4096,256]{0,1:T(8,128)S(1)} %copy-done, f32[4096,4096]{0,1:T(8,128)} %bitcast_multiply_fusion, f32[8,4096]{1,0:T(8,128)S(1)} %reshape.286, f32[8]{0:T(128)S(1)} %add_rsqrt_fusion, f32[4096]{0:T(1024)S(1)} %copy-done.8), kind=kOutput, calls=%fused_computation.4 | convolution fusion | flops 1849753600 | bytes 75792416 | tf_op jit(solution)/shard_map/dot_general | solution.py:75
  451.4 36.3 %all-reduce.5.cloned.1.call-done = (f32[8,4608]{1,0:T(8,128)}, f32[8,4608]{1,0:T(8,128)}) async-done(((f32[8,4608]{1,0:T(8,128)}, f32[8,4608]{1,0:T(8,128)}), (f32[8,4608]{1,0:T(8,128)}, f32[8,4608]{1,0:T(8,128)})) %all-reduce.5.cloned.1.call-update) | async-done | bytes 294928
  487.6 0.8 dynamic-slice.8
  488.4 0.8 dynamic-slice.5
  489.2 0.8 dynamic-slice.14
  489.9 0.8 dynamic-slice.15
  490.7 0.9 dynamic-slice_bitcast_fusion.1
  491.6 0.9 dynamic-slice_bitcast_fusion
  493.1 2.4 fusion.19
  496.0 1.6 convolution_convert_fusion.1
  497.6 14.0 %all-gather = bf16[8,2,4096]{2,1,0:T(2,128)(2,1)S(1)} all-gather(bf16[1,2,4096]{2,1,0:T(2,128)(2,1)S(1)} %reshape.293), channel_id=1, replica_groups=mesh['groups'=2,'width'=4,'hidden'=2,'batch'=2] {'width','batch'}, dimensions={0}, use_global_device_ids=true | all-gather | bytes 147456 | tf_op jit(solution)/shard_map/all_gather | solution.py:112
  511.6 13.8 %fusion.48 = f32[16,4096]{1,0:T(8,128)} fusion(bf16[16,4096]{1,0:T(8,128)(2,1)S(1)} %reshape.294, bf16[4096,4096]{1,0:T(8,128)(2,1)} %param.16), kind=kOutput, calls=%fused_computation.100 | convolution fusion | flops 536870912 | bytes 33947648 | tf_op jit(solution)/shard_map/dot_general | solution.py:111
  526.2 1.6 convolution_convert_fusion
  527.8 14.0 %all-gather.1 = bf16[8,2,4096]{2,1,0:T(2,128)(2,1)S(1)} all-gather(bf16[1,2,4096]{2,1,0:T(2,128)(2,1)S(1)} %reshape.295), channel_id=1, replica_groups=mesh['groups'=2,'width'=4,'hidden'=2,'batch'=2] {'width','batch'}, dimensions={0}, use_global_device_ids=true | all-gather | bytes 147456 | tf_op jit(solution)/shard_map/all_gather | solution.py:112
  541.8 13.5 %fusion.49 = f32[16,4096]{1,0:T(8,128)} fusion(bf16[16,4096]{1,0:T(8,128)(2,1)S(1)} %reshape.296, bf16[4096,4096]{1,0:T(8,128)(2,1)} %param.16), kind=kOutput, calls=%fused_computation.101 | convolution fusion | flops 536870912 | bytes 33947648 | tf_op jit(solution)/shard_map/dot_general | solution.py:111
  555.4 0.9 fusion.30
  556.3 10.7 %reduce-scatter.5.cloned.1.call-done = f32[8,4096]{1,0:T(8,128)} async-done(((f32[16,4096]{1,0:T(8,128)}), f32[8,4096]{1,0:T(8,128)}) %reduce-scatter.5.cloned.1.call-update) | async-done | bytes 131088 | tf_op jit(solution)/shard_map/reduce_scatter | solution.py:117
  567.0 0.9 fusion.31
  (73 shorter events, 9.4 us)
Async XLA Ops:
  6.5 481.1 %all-reduce.5.cloned.1.call-start = ((), (), s32[]{:S(2)}) async-start(), calls=%async_computation.4 | async-start | bytes 589824
  8.7 291.8 %collective-permute-start = (f32[8]{0:T(128)}, f32[8]{0:T(128)}, u32[]{:S(2)}, u32[]{:S(2)}) collective-permute-start(f32[8]{0:T(128)} %reduce_sum.41), channel_id=1, source_target_pairs={{0,4},{4,0},{8,12},{12,8},{1,5},{5,1},{9,13},{13,9},{2,6},{6,2},{1... | collective-permute-start | bytes 104 | tf_op jit(solution)/shard_map/ppermute | solution.py:72
  12.3 292.1 %collective-permute-start.2 = (f32[8]{0:T(128)}, f32[8]{0:T(128)}, u32[]{:S(2)}, u32[]{:S(2)}) collective-permute-start(f32[8]{0:T(128)} %reduce_sum.44), channel_id=1, source_target_pairs={{0,4},{4,0},{8,12},{12,8},{1,5},{5,1},{9,13},{13,9},{2,6},{6,2},{1... | collective-permute-start | bytes 104 | tf_op jit(solution)/shard_map/ppermute | solution.py:72
  84.5 78.3 %copy-start.4 = (f32[32,4096]{1,0:T(8,128)S(1)}, f32[32,4096]{1,0:T(8,128)}, u32[]{:S(2)}) copy-start(f32[32,4096]{1,0:T(8,128)} %param.13) | copy-start | bytes 1572868
  84.5 95.9 %copy-start.6 = (s32[2]{0:T(128)S(1)}, s32[2]{0:T(128)}, u32[]{:S(2)}) copy-start(s32[2]{0:T(128)} %param.19) | copy-start | bytes 28
  221.5 84.4 %copy-start.5 = (f32[8,4096]{1,0:T(8,128)S(1)}, f32[8,4096]{1,0:T(8,128)}, u32[]{:S(2)}) copy-start(f32[8,4096]{1,0:T(8,128)} %reshape.281) | copy-start | bytes 393220
  221.5 84.4 %copy-start.8 = (f32[4096]{0:T(1024)S(1)}, f32[4096]{0:T(1024)}, u32[]{:S(2)}) copy-start(f32[4096]{0:T(1024)} %param.11) | copy-start | bytes 49156
  300.5 84.1 %copy-start = (f32[4096,256]{0,1:T(8,128)S(1)}, f32[4096,256]{0,1:T(8,128)}, u32[]{:S(2)}) copy-start(f32[4096,256]{0,1:T(8,128)} %convert_element_type.85) | copy-start | bytes 12582916
  300.5 84.1 %copy-start.1 = (f32[4096,256]{0,1:T(8,128)S(1)}, f32[4096,256]{0,1:T(8,128)}, u32[]{:S(2)}) copy-start(f32[4096,256]{0,1:T(8,128)} %convert_element_type.86) | copy-start | bytes 12582916
  301.3 4.6 collective-permute-start.1
  305.1 79.4 %collective-permute-start.3 = (f32[8]{0:T(128)S(1)}, f32[8]{0:T(128)S(1)}, u32[]{:S(2)}, u32[]{:S(2)}) collective-permute-start(f32[8]{0:T(128)S(1)} %add.61), channel_id=1, source_target_pairs={{0,8},{4,12},{8,0},{12,4},{1,9},{5,13},{9,1},{13,5},{2,10},{6,14},... | collective-permute-start | bytes 104 | tf_op jit(solution)/shard_map/ppermute | solution.py:72
  384.5 65.4 %copy-start.7 = (f32[64]{0:T(128)S(1)}, f32[64]{0:T(128)}, u32[]{:S(2)}) copy-start(f32[64]{0:T(128)} %multiply_power_fusion) | copy-start | bytes 772
  384.5 65.5 %copy-start.9 = (u32[32]{0:T(128)S(1)}, u32[32]{0:T(128)}, u32[]{:S(2)}) copy-start(u32[32]{0:T(128)} %constant.51) | copy-start | bytes 388
  384.5 108.5 %copy-start.2 = (bf16[2,1024,256]{2,1,0:T(8,128)(2,1)S(1)}, bf16[2,1024,256]{2,1,0:T(8,128)(2,1)}, u32[]{:S(2)}) copy-start(bf16[2,1024,256]{2,1,0:T(8,128)(2,1)} %param.18) | copy-start | bytes 3145732
  384.5 108.5 %copy-start.3 = (bf16[2,1024,256]{2,1,0:T(8,128)(2,1)S(1)}, bf16[2,1024,256]{2,1,0:T(8,128)(2,1)}, u32[]{:S(2)}) copy-start(bf16[2,1024,256]{2,1,0:T(8,128)(2,1)} %param.17) | copy-start | bytes 3145732
  449.8 105.6 %reduce-scatter.3.cloned.1.call-start = ((), (), s32[]{:S(2)}) async-start(), calls=%async_computation.2 | async-start | bytes 393216 | tf_op jit(solution)/shard_map/reduce_scatter | solution.py:117
  525.4 41.6 %reduce-scatter.5.cloned.1.call-start = ((), (), s32[]{:S(2)}) async-start(), calls=%async_computation.3 | async-start | bytes 393216 | tf_op jit(solution)/shard_map/reduce_scatter | solution.py:117
Sparse Core Ops, SparseCore 0:
  449.9 37.6 all-reduce.4
  525.6 11.4 reduce-scatter.2
  555.5 11.4 reduce-scatter.4
